TPU v7x, 32 devices: a whole 2x2x4 slice. The times are simulated.
32 devices in a mesh: dp: 16 (over z, y, x), mp: 2 (over core).
Axes of the slice: x: 2, y: 2, z: 4, core: 2. Of those that a mesh axis runs over, the one named last changes fastest.
Arguments:
- tokens: bfloat16 [32768, 768], P(('dp', 'mp')), may hold values from -6 to 6
- out_grad: bfloat16 [32768, 768], P(('dp', 'mp')), may hold values from -6 to 6
- image_lengths: int32 [16, 69], P('dp'), may hold values from 0 to 98, as said below
- group_of_block: int32 [16], P('dp'), may hold values from 0 to 2, as said below
- norm_gains: float32 [2, 768], replicated, may hold values from 0.5 to 1.5
- row_biases: float32 [4, 768], replicated, may hold values from -1.5 to 1.5
- w_qkv: bfloat16 [3, 768, 768], P(None, None, 'mp'), may hold values from -0.21875 to 0.21875
- qv_bias: float32 [2, 768], P(None, 'mp'), may hold values from -1.5 to 1.5
- w_out: bfloat16 [768, 768], P('mp'), may hold values from -0.875 to 0.875
- w_fc1: bfloat16 [768, 3072], P(None, 'mp'), may hold values from -0.21875 to 0.21875
- b_fc1: float32 [3072], P('mp'), may hold values from -1.5 to 1.5
- w_fc2: bfloat16 [3072, 768], P('mp'), may hold values from -0.109375 to 0.109375
Outputs:
- output: bfloat16 [32768, 768], P(('dp', 'mp'))
- tokens_grad: float32 [32768, 768], P(('dp', 'mp'))
- norm_gains_grad: float32 [2, 768], replicated
- row_biases_grad: float32 [4, 768], replicated
- w_qkv_grad: float32 [3, 768, 768], P(None, None, 'mp')
- qv_bias_grad: float32 [2, 768], P(None, 'mp')
- w_out_grad: float32 [768, 768], P('mp')
- w_fc1_grad: float32 [768, 3072], P(None, 'mp')
- b_fc1_grad: float32 [3072], P('mp')
- w_fc2_grad: float32 [3072, 768], P('mp')
Inputs may be any that keep to these rules, and one draw needn't show every extreme that they name: `image_lengths`: row b lists the patch counts of the images packed in block b from the first slot on; each image has 30 to 98 patches, slots after the last image hold 0, the counts of a row sum to at most 2048 and the rest of the block is padding; every block has an image of 98 patches. `group_of_block`: entry b is the dataset group of block b; it never falls along the blocks, and each of the 3 groups holds at least one block.
All inputs are finite; a program needn't handle non-finite values.
Results may differ from a plain program's by a relative error of at most 0.015.
Values may be sent and summed in bfloat16 or wider, within the bound.
No kernel may reach another device: no remote copies, remote signals or barrier semaphores. Data moves between devices by JAX's collectives and lax.ppermute only.
A program may use at most 256 MiB of HBM per device.

v0:
```python
import jax
import jax.numpy as jnp
from jax import lax
from jax.sharding import PartitionSpec as P

HEAD_DIM = 64
GROUPS = 3
LEN_NORM = 64


def layer_norm(values, gain_vec, shift_vec):
    center = values - jnp.mean(values, axis=-1, keepdims=True)
    spread = jnp.mean(center * center, axis=-1, keepdims=True)
    return center * lax.rsqrt(spread + 1e-06) * gain_vec + shift_vec


def gelu_tanh(values):
    return (
        0.5
        * values
        * (1.0 + jnp.tanh(0.7978845608028654 * (values + 0.044715 * values * values * values)))
    )


def image_rows(lengths, row_count):
    image_ends = jnp.cumsum(lengths)
    position = jnp.arange(row_count, dtype=jnp.int32)
    segment = jnp.sum((position[:, None] >= image_ends[None, :]).astype(jnp.int32), axis=1)
    slot_ids = jnp.arange(lengths.shape[0], dtype=jnp.int32)
    row_length = jnp.sum(
        jnp.where(segment[:, None] == slot_ids[None, :], lengths[None, :], 0), axis=1
    )
    return (segment, row_length)


def score_block(query_block, segment_block, keys_all, segment, score_scale):
    scores = (
        jnp.einsum("qhd,khd->hqk", query_block, keys_all, preferred_element_type=jnp.float32)
        * score_scale
    )
    return jnp.where((segment_block[:, None] == segment[None, :])[None], scores, -1000000000.0)


def local(
    tokens,
    out_grad,
    image_lengths,
    group_of_block,
    norm_gains,
    row_biases,
    w_qkv,
    qv_bias,
    w_out,
    w_fc1,
    b_fc1,
    w_fc2,
):
    own_rows = tokens.shape[0]
    row_count = own_rows * lax.axis_size("mp")
    first_row = lax.axis_index("mp") * own_rows
    segment, row_length = image_rows(image_lengths[0], row_count)
    images = jnp.sum((image_lengths[0] > 0).astype(jnp.float32))
    member = (group_of_block[0] == jnp.arange(GROUPS, dtype=jnp.int32)).astype(jnp.float32)
    group_images = lax.psum(member * images, "dp")
    group_roots = jnp.sqrt(group_images)
    factor = jnp.sum(group_images) / (group_roots * jnp.sum(group_roots))
    block_factor = jnp.sum(member * factor)
    own_length = lax.dynamic_slice_in_dim(row_length, first_row, own_rows)
    weight_row = (
        block_factor
        * LEN_NORM
        * (own_length > 0).astype(jnp.float32)
        / jnp.maximum(own_length, 1).astype(jnp.float32)
    )
    tokens_f = tokens.astype(jnp.float32)
    normed, norm_pull = jax.vjp(layer_norm, tokens_f, norm_gains[0], row_biases[0])
    normed_low = normed.astype(jnp.bfloat16)
    normed_all = lax.all_gather(normed_low, "mp", axis=0, tiled=True)
    projected = jnp.einsum("rd,tde->tre", normed_all, w_qkv, preferred_element_type=jnp.float32)
    bias_three = jnp.stack([qv_bias[0], jnp.zeros_like(qv_bias[0]), qv_bias[1]])
    projected = (projected + bias_three[:, None, :]).astype(jnp.bfloat16)
    local_width = w_qkv.shape[2]
    head_count = local_width // HEAD_DIM
    shaped = projected.reshape(3, row_count, head_count, HEAD_DIM)
    queries, keys_all, values_all = (shaped[0], shaped[1], shaped[2])
    block_rows = min(512, row_count)
    block_count = row_count // block_rows
    score_scale = HEAD_DIM ** (-0.5)
    query_blocks = queries.reshape(block_count, block_rows, head_count, HEAD_DIM)
    segment_blocks = segment.reshape(block_count, block_rows)

    def forward_block(pieces):
        query_block, segment_block = pieces
        scores = score_block(query_block, segment_block, keys_all, segment, score_scale)
        top_score = jnp.max(scores, axis=-1, keepdims=True)
        exponent = jnp.exp(scores - top_score)
        total = jnp.sum(exponent, axis=-1, keepdims=True)
        weights = (exponent / total).astype(jnp.bfloat16)
        context = jnp.einsum(
            "hqk,khd->qhd", weights, values_all, preferred_element_type=jnp.float32
        )
        return (context, (top_score + jnp.log(total))[:, :, 0])

    context, log_total = lax.map(forward_block, (query_blocks, segment_blocks))
    context_low = context.reshape(row_count, local_width).astype(jnp.bfloat16)
    piece = context_low
    attention = lax.psum_scatter(
        jnp.dot(piece, w_out, preferred_element_type=jnp.float32).astype(jnp.bfloat16),
        "mp",
        scatter_dimension=0,
        tiled=True,
    ).astype(jnp.float32)
    hidden_one = tokens_f + attention + row_biases[2]
    normed_two, norm_two_pull = jax.vjp(layer_norm, hidden_one, norm_gains[1], row_biases[1])
    normed_two_all = lax.all_gather(normed_two.astype(jnp.bfloat16), "mp", axis=0, tiled=True)
    before = jnp.dot(normed_two_all, w_fc1, preferred_element_type=jnp.float32) + b_fc1
    activated, gelu_pull = jax.vjp(gelu_tanh, before)
    activated_low = activated.astype(jnp.bfloat16)
    piece = activated_low
    mlp_out = lax.psum_scatter(
        jnp.dot(piece, w_fc2, preferred_element_type=jnp.float32).astype(jnp.bfloat16),
        "mp",
        scatter_dimension=0,
        tiled=True,
    ).astype(jnp.float32)
    output = (hidden_one + mlp_out + row_biases[3]).astype(jnp.bfloat16)
    out_cot = out_grad.astype(jnp.float32) * weight_row[:, None]
    out_cot_all = lax.all_gather(out_cot.astype(jnp.bfloat16), "mp", axis=0, tiled=True)
    grad_fc2 = jnp.einsum(
        "rf,rd->fd", activated_low, out_cot_all, preferred_element_type=jnp.float32
    )
    grad_act = jnp.einsum("rd,fd->rf", out_cot_all, w_fc2, preferred_element_type=jnp.float32)
    grad_before = gelu_pull(grad_act)[0].astype(jnp.bfloat16)
    grad_bfc1 = jnp.sum(grad_before.astype(jnp.float32), axis=0)
    grad_fc1 = jnp.einsum(
        "rd,rf->df", normed_two_all, grad_before, preferred_element_type=jnp.float32
    )
    piece = grad_before
    grad_norm_two = lax.psum_scatter(
        jnp.einsum("rf,df->rd", piece, w_fc1, preferred_element_type=jnp.float32).astype(
            jnp.bfloat16
        ),
        "mp",
        scatter_dimension=0,
        tiled=True,
    ).astype(jnp.float32)
    grad_hidden, grad_gain_two, grad_shift_two = norm_two_pull(grad_norm_two)
    grad_hidden = grad_hidden + out_cot
    grad_hidden_all = lax.all_gather(grad_hidden.astype(jnp.bfloat16), "mp", axis=0, tiled=True)
    grad_out = jnp.einsum(
        "rc,rd->cd", context_low, grad_hidden_all, preferred_element_type=jnp.float32
    )
    grad_context = jnp.einsum(
        "rd,cd->rc", grad_hidden_all, w_out, preferred_element_type=jnp.float32
    ).astype(jnp.bfloat16)
    context_blocks = grad_context.reshape(block_count, block_rows, head_count, HEAD_DIM)

    def backward_block(carry, pieces):
        grad_keys, grad_values = carry
        query_block, segment_block, log_block, grad_block = pieces
        scores = score_block(query_block, segment_block, keys_all, segment, score_scale)
        probs = jnp.exp(scores - log_block[:, :, None])
        grad_values = grad_values + jnp.einsum(
            "hqk,qhd->khd",
            probs.astype(jnp.bfloat16),
            grad_block,
            preferred_element_type=jnp.float32,
        )
        grad_probs = jnp.einsum(
            "qhd,khd->hqk", grad_block, values_all, preferred_element_type=jnp.float32
        )
        grad_scores = probs * (grad_probs - jnp.sum(probs * grad_probs, axis=-1, keepdims=True))
        grad_scores = grad_scores.astype(jnp.bfloat16)
        grad_query = (
            jnp.einsum("hqk,khd->qhd", grad_scores, keys_all, preferred_element_type=jnp.float32)
            * score_scale
        )
        grad_keys = (
            grad_keys
            + jnp.einsum(
                "hqk,qhd->khd", grad_scores, query_block, preferred_element_type=jnp.float32
            )
            * score_scale
        )
        return ((grad_keys, grad_values), grad_query)

    zero_heads = jnp.zeros((row_count, head_count, HEAD_DIM), jnp.float32)
    (grad_keys, grad_values), grad_queries = lax.scan(
        backward_block,
        (zero_heads, zero_heads),
        (query_blocks, segment_blocks, log_total, context_blocks),
    )
    grad_projected = jnp.stack(
        [
            grad_queries.reshape(row_count, local_width),
            grad_keys.reshape(row_count, local_width),
            grad_values.reshape(row_count, local_width),
        ]
    ).astype(jnp.bfloat16)
    grad_qv_bias = jnp.stack(
        [
            jnp.sum(grad_projected[0].astype(jnp.float32), axis=0),
            jnp.sum(grad_projected[2].astype(jnp.float32), axis=0),
        ]
    )
    grad_qkv = jnp.einsum(
        "rd,tre->tde", normed_all, grad_projected, preferred_element_type=jnp.float32
    )
    piece = grad_projected
    grad_norm_one = lax.psum_scatter(
        jnp.einsum("tre,tde->rd", piece, w_qkv, preferred_element_type=jnp.float32).astype(
            jnp.bfloat16
        ),
        "mp",
        scatter_dimension=0,
        tiled=True,
    ).astype(jnp.float32)
    grad_input, grad_gain_one, grad_shift_one = norm_pull(grad_norm_one)
    grad_input = grad_input + grad_hidden
    gain_grads, shift_grads = lax.psum(
        (
            jnp.stack([grad_gain_one, grad_gain_two]),
            jnp.stack(
                [
                    grad_shift_one,
                    grad_shift_two,
                    jnp.sum(grad_hidden, axis=0),
                    jnp.sum(out_cot, axis=0),
                ]
            ),
        ),
        ("dp", "mp"),
    )
    grad_qkv, grad_qv_bias, grad_out, grad_fc1, grad_bfc1, grad_fc2 = lax.psum(
        (grad_qkv, grad_qv_bias, grad_out, grad_fc1, grad_bfc1, grad_fc2), "dp"
    )
    return (
        output,
        grad_input,
        gain_grads,
        shift_grads,
        grad_qkv,
        grad_qv_bias,
        grad_out,
        grad_fc1,
        grad_bfc1,
        grad_fc2,
    )


def solution(mesh):
    placed = (
        P(("dp", "mp"), None),
        P(("dp", "mp"), None),
        P("dp", None),
        P("dp"),
        P(),
        P(),
        P(None, None, "mp"),
        P(None, "mp"),
        P("mp", None),
        P(None, "mp"),
        P("mp"),
        P("mp", None),
    )
    return jax.shard_map(
        local,
        mesh=mesh,
        in_specs=placed,
        out_specs=(
            P(("dp", "mp"), None),
            P(("dp", "mp"), None),
            P(),
            P(),
            P(None, None, "mp"),
            P(None, "mp"),
            P("mp", None),
            P(None, "mp"),
            P("mp"),
            P("mp", None),
        ),
        check_vma=False,
    )
```

profile of v0, /device:TPU:0, one launch (start us, length us, event | category | flops | bytes accessed | tf_op | source)
XLA Modules:
  0.0 1192.0 jit_solution(15143467741998065962)
XLA Ops:
  15.6 14.2 %all-gather.5.cloned.1.call-done = bf16[2048,768]{1,0:T(8,128)(2,1)} async-done(((bf16[1024,768]{1,0:T(8,128)(2,1)}), bf16[2048,768]{1,0:T(8,128)(2,1)}) %all-gather.5.cloned.1.call-update) | async-done | bytes 3145744 | tf_op jit(solution)/shard_map/all_gather | solution.py:78
  29.8 6.3 fusion.45
  38.5 4.0 reshape_squeeze.3
  46.7 159.6 %while.27 = (s32[]{:T(128)}, bf16[4,512,6,64]{1,3,2,0:T(8,128)(2,1)}, f32[4,6,512]{2,1,0:T(8,128)S(1)}, s32[4,512]{1,0:T(4,128)S(1)}, s32[2048]{0:T(1024)S(1)}, ...) while((s32[]{:T(128)}, ...), condition=%wide.region_7.8_spmd, body=%wide.region_4.7_spmd.sunk | while | flops 1687155712 | bytes 103024832 | solution.py:104
  47.3 14.3 %fusion.128 = (f32[6,512]{1,0:T(8,128)S(1)}, f32[6,512,2048]{2,1,0:T(8,128)}) fusion(pred[512,2048]{1,0:T(8,128)(4,1)S(1)} %broadcast_compare_fusion.4, bf16[2048,6,64]{0,2,1:T(8,128)(2,1)} %get-tuple-element.469, bf16[4,512,6,64]{1,3,2,0:T(8,128)(2,1)} %get-tuple-element.468, s32[]{:T(128)S(6)} %copy.67), kind=kOutput, calls=%fused_computation.3.clone.1 | convolution fusion | flops 824177664 | bytes 28192772 | tf_op jit(solution)/shard_map/while/body/eval_jaxpr/qhd,khd->hqk/dot_general | solution.py:38
  61.6 12.1 %fusion.129 = f32[6,512]{1,0:T(8,128)S(1)} fusion(f32[6,512,2048]{2,1,0:T(8,128)} %get-tuple-element.430, f32[6,512]{1,0:T(8,128)S(1)} %get-tuple-element.431, pred[512,2048]{1,0:T(8,128)(4,1)S(1)} %broadcast_compare_fusion.4), kind=kLoop, calls=%fused_computation.4.clone.1 | loop fusion | flops 25162752 | bytes 26238976 | tf_op jit(solution)/shard_map/while/body/eval_jaxpr/reduce_sum | solution.py:97
  73.7 11.6 fusion.130
  87.2 14.3 %fusion.128 = (f32[6,512]{1,0:T(8,128)S(1)}, f32[6,512,2048]{2,1,0:T(8,128)}) fusion(pred[512,2048]{1,0:T(8,128)(4,1)S(1)} %broadcast_compare_fusion.4, bf16[2048,6,64]{0,2,1:T(8,128)(2,1)} %get-tuple-element.469, bf16[4,512,6,64]{1,3,2,0:T(8,128)(2,1)} %get-tuple-element.468, s32[]{:T(128)S(6)} %copy.67), kind=kOutput, calls=%fused_computation.3.clone.1 | convolution fusion | flops 824177664 | bytes 28192772 | tf_op jit(solution)/shard_map/while/body/eval_jaxpr/qhd,khd->hqk/dot_general | solution.py:38
  101.5 12.1 %fusion.129 = f32[6,512]{1,0:T(8,128)S(1)} fusion(f32[6,512,2048]{2,1,0:T(8,128)} %get-tuple-element.430, f32[6,512]{1,0:T(8,128)S(1)} %get-tuple-element.431, pred[512,2048]{1,0:T(8,128)(4,1)S(1)} %broadcast_compare_fusion.4), kind=kLoop, calls=%fused_computation.4.clone.1 | loop fusion | flops 25162752 | bytes 26238976 | tf_op jit(solution)/shard_map/while/body/eval_jaxpr/reduce_sum | solution.py:97
  113.6 11.6 fusion.130
  127.1 14.3 %fusion.128 = (f32[6,512]{1,0:T(8,128)S(1)}, f32[6,512,2048]{2,1,0:T(8,128)}) fusion(pred[512,2048]{1,0:T(8,128)(4,1)S(1)} %broadcast_compare_fusion.4, bf16[2048,6,64]{0,2,1:T(8,128)(2,1)} %get-tuple-element.469, bf16[4,512,6,64]{1,3,2,0:T(8,128)(2,1)} %get-tuple-element.468, s32[]{:T(128)S(6)} %copy.67), kind=kOutput, calls=%fused_computation.3.clone.1 | convolution fusion | flops 824177664 | bytes 28192772 | tf_op jit(solution)/shard_map/while/body/eval_jaxpr/qhd,khd->hqk/dot_general | solution.py:38
  141.3 12.1 %fusion.129 = f32[6,512]{1,0:T(8,128)S(1)} fusion(f32[6,512,2048]{2,1,0:T(8,128)} %get-tuple-element.430, f32[6,512]{1,0:T(8,128)S(1)} %get-tuple-element.431, pred[512,2048]{1,0:T(8,128)(4,1)S(1)} %broadcast_compare_fusion.4), kind=kLoop, calls=%fused_computation.4.clone.1 | loop fusion | flops 25162752 | bytes 26238976 | tf_op jit(solution)/shard_map/while/body/eval_jaxpr/reduce_sum | solution.py:97
  153.5 11.6 fusion.130
  166.9 14.3 %fusion.128 = (f32[6,512]{1,0:T(8,128)S(1)}, f32[6,512,2048]{2,1,0:T(8,128)}) fusion(pred[512,2048]{1,0:T(8,128)(4,1)S(1)} %broadcast_compare_fusion.4, bf16[2048,6,64]{0,2,1:T(8,128)(2,1)} %get-tuple-element.469, bf16[4,512,6,64]{1,3,2,0:T(8,128)(2,1)} %get-tuple-element.468, s32[]{:T(128)S(6)} %copy.67), kind=kOutput, calls=%fused_computation.3.clone.1 | convolution fusion | flops 824177664 | bytes 28192772 | tf_op jit(solution)/shard_map/while/body/eval_jaxpr/qhd,khd->hqk/dot_general | solution.py:38
  181.2 12.1 %fusion.129 = f32[6,512]{1,0:T(8,128)S(1)} fusion(f32[6,512,2048]{2,1,0:T(8,128)} %get-tuple-element.430, f32[6,512]{1,0:T(8,128)S(1)} %get-tuple-element.431, pred[512,2048]{1,0:T(8,128)(4,1)S(1)} %broadcast_compare_fusion.4), kind=kLoop, calls=%fused_computation.4.clone.1 | loop fusion | flops 25162752 | bytes 26238976 | tf_op jit(solution)/shard_map/while/body/eval_jaxpr/reduce_sum | solution.py:97
  193.3 11.6 fusion.130
  210.6 3.5 convolution_convert_fusion
  214.2 12.2 %reduce-scatter.5.cloned.1.call-done = bf16[1024,768]{1,0:T(8,128)(2,1)} async-done(((bf16[2048,768]{1,0:T(8,128)(2,1)}), bf16[1024,768]{1,0:T(8,128)(2,1)}) %reduce-scatter.5.cloned.1.call-update) | async-done | bytes 1572880 | tf_op jit(solution)/shard_map/reduce_scatter | solution.py:107
  234.2 41.9 %psum.63 = f32[3]{0:T(128)S(1)} all-reduce(f32[3]{0:T(128)S(1)} %compare_select_fusion.1), channel_id=1, replica_groups=mesh['dp'=16,'mp'=2] {'dp'}, use_global_device_ids=true, to_apply=%region_14.15 | all-reduce | flops 3 | bytes 24 | tf_op jit(solution)/shard_map/psum | solution.py:64
  282.4 13.7 %multiply_convert_fusion.1 = (bf16[2048,1536]{1,0:T(8,128)(2,1)}, f32[2048,1536]{1,0:T(8,128)}) fusion(f32[1536]{0:T(1024)S(1)} %copy-done.48, bf16[2048,768]{1,0:T(8,128)(2,1)} %all-gather.7.cloned.1.call-done, bf16[768,1536]{1,0:T(8,128)(2,1)S(1)} %copy-done), kind=kOutput, calls=%fused_computation.58 | convolution fusion | flops 4863295488 | bytes 24385536 | tf_op jit(solution)/shard_map/dot_general | solution.py:116
  296.1 19.5 %convert_reduce_fusion = (f32[1536]{0:T(1024)}, bf16[2048,1536]{1,0:T(8,128)(2,1)S(1)}) fusion(bf16[2048,768]{1,0:T(8,128)(2,1)} %all-gather.9.cloned.1.call-done, bf16[1536,768]{1,0:T(8,128)(2,1)} %param.27, f32[2048,1536]{1,0:T(8,128)} %get-tuple-element.318, f32[1536]{0:T(1024)S(1)} %copy-done.48), kind=kOutput, calls=%fused_computation.57 | convolution fusion | flops 4916771328 | bytes 24391680 | tf_op jit(solution)/shard_map/rd,fd->rf/dot_general | solution.py:132
  318.2 6.4 convolution_convert_fusion.1
  326.3 9.7 convolution_convert_fusion.2
  337.4 3.9 convert_reduce_fusion.2
  341.3 4.2 fusion.56
  346.4 5.6 fusion.77
  355.0 13.4 %all-gather.11.cloned.1.call-done = bf16[2048,768]{1,0:T(8,128)(2,1)} async-done(((bf16[1024,768]{1,0:T(8,128)(2,1)}), bf16[2048,768]{1,0:T(8,128)(2,1)}) %all-gather.11.cloned.1.call-update) | async-done | bytes 3145744 | tf_op jit(solution)/shard_map/all_gather | solution.py:149
  368.4 4.9 convolution_convert_fusion.3
  381.7 333.3 %while.28 = (s32[]{:T(128)}, f32[2048,6,64]{0,2,1:T(8,128)}, f32[2048,6,64]{0,2,1:T(8,128)}, bf16[4,512,6,64]{1,3,2,0:T(8,128)(2,1)}, bf16[4,512,6,64]{1,3,2,0:T...) while((s32[]{:T(128)}, f32[2048,6,64]{0,2,1:T(8,128)}, ...), condition=%wide.region_23.24_spmd.clone, body=%wide.region_21.23_spmd.clone.sunk | while | flops 4126077952 | bytes 212699312 | solution.py:188
  382.6 11.0 fusion.140
  393.7 12.8 %bitcast_add_fusion.5 = f32[2048,6,64]{0,2,1:T(8,128)} fusion(f32[2048,6,64]{0,2,1:T(8,128)} %get-tuple-element.487, f32[6,512,2048]{2,1,0:T(8,128)} %fusion.140, f32[6,512]{1,0:T(8,128)S(1)} %dynamic-slice_bitcast_fusion.2, pred[512,2048]{1,0:T(8,128)(4,1)S(1)} %broadcast_compare_fusion.5, pred[]{:T(512)S(6)} %compare.3, ...), kind=kOutput, calls=%fused_computation.23.clone.1 | convolution fusion | flops 832045056 | bytes 32911364 | tf_op jit(solution)/shard_map/while/body/eval_jaxpr/hqk,qhd->khd/dot_general | solution.py:163
  406.5 18.1 %multiply_reduce_fusion.3 = (f32[6,512]{1,0:T(8,128)S(1)}, f32[6,512,2048]{2,1,0:T(8,128)}) fusion(f32[6,512,2048]{2,1,0:T(8,128)} %fusion.140, f32[6,512]{1,0:T(8,128)S(1)} %dynamic-slice_bitcast_fusion.2, pred[512,2048]{1,0:T(8,128)(4,1)S(1)} %broadcast_compare_fusion.5, bf16[2048,6,64]{0,2,1:T(8,128)(2,1)} %get-tuple-element.508, ...), kind=kOutput, calls=%fused_computation.18.clone.1 | convolution fusion | flops 836760576 | bytes 53370884 | tf_op jit(solution)/shard_map/while/body/eval_jaxpr/qhd,khd->hqk/dot_general | solution.py:169
  424.6 21.3 %multiply_convert_fusion.3 = bf16[6,512,2048]{2,1,0:T(8,128)(2,1)} fusion(f32[6,512,2048]{2,1,0:T(8,128)} %get-tuple-element.443, f32[6,512,2048]{2,1,0:T(8,128)} %fusion.140, f32[6,512]{1,0:T(8,128)S(1)} %get-tuple-element.444, f32[6,512]{1,0:T(8,128)S(1)} %dynamic-slice_bitcast_fusion.2, pred[512,2048]{1,0:T(8,128)(4,1)S(1)} %broadcast_compare_fusion.5), kind=kLoop, calls=%fused_computation.17.clone.1 | loop fusion | flops 37748736 | bytes 63987712 | tf_op jit(solution)/shard_map/while/body/eval_jaxpr/convert_element_type | solution.py:173
  445.8 9.3 fusion.141
  455.1 8.7 bitcast_add_fusion.4
  464.5 11.0 fusion.140
  475.5 13.7 %bitcast_add_fusion.5 = f32[2048,6,64]{0,2,1:T(8,128)} fusion(f32[2048,6,64]{0,2,1:T(8,128)} %get-tuple-element.487, f32[6,512,2048]{2,1,0:T(8,128)} %fusion.140, f32[6,512]{1,0:T(8,128)S(1)} %dynamic-slice_bitcast_fusion.2, pred[512,2048]{1,0:T(8,128)(4,1)S(1)} %broadcast_compare_fusion.5, pred[]{:T(512)S(6)} %compare.3, ...), kind=kOutput, calls=%fused_computation.23.clone.1 | convolution fusion | flops 832045056 | bytes 32911364 | tf_op jit(solution)/shard_map/while/body/eval_jaxpr/hqk,qhd->khd/dot_general | solution.py:163
  489.2 18.1 %multiply_reduce_fusion.3 = (f32[6,512]{1,0:T(8,128)S(1)}, f32[6,512,2048]{2,1,0:T(8,128)}) fusion(f32[6,512,2048]{2,1,0:T(8,128)} %fusion.140, f32[6,512]{1,0:T(8,128)S(1)} %dynamic-slice_bitcast_fusion.2, pred[512,2048]{1,0:T(8,128)(4,1)S(1)} %broadcast_compare_fusion.5, bf16[2048,6,64]{0,2,1:T(8,128)(2,1)} %get-tuple-element.508, ...), kind=kOutput, calls=%fused_computation.18.clone.1 | convolution fusion | flops 836760576 | bytes 53370884 | tf_op jit(solution)/shard_map/while/body/eval_jaxpr/qhd,khd->hqk/dot_general | solution.py:169
  507.3 21.3 %multiply_convert_fusion.3 = bf16[6,512,2048]{2,1,0:T(8,128)(2,1)} fusion(f32[6,512,2048]{2,1,0:T(8,128)} %get-tuple-element.443, f32[6,512,2048]{2,1,0:T(8,128)} %fusion.140, f32[6,512]{1,0:T(8,128)S(1)} %get-tuple-element.444, f32[6,512]{1,0:T(8,128)S(1)} %dynamic-slice_bitcast_fusion.2, pred[512,2048]{1,0:T(8,128)(4,1)S(1)} %broadcast_compare_fusion.5), kind=kLoop, calls=%fused_computation.17.clone.1 | loop fusion | flops 37748736 | bytes 63987712 | tf_op jit(solution)/shard_map/while/body/eval_jaxpr/convert_element_type | solution.py:173
  528.6 9.3 fusion.141
  537.8 9.6 bitcast_add_fusion.4
  548.1 11.0 fusion.140
  559.1 13.7 %bitcast_add_fusion.5 = f32[2048,6,64]{0,2,1:T(8,128)} fusion(f32[2048,6,64]{0,2,1:T(8,128)} %get-tuple-element.487, f32[6,512,2048]{2,1,0:T(8,128)} %fusion.140, f32[6,512]{1,0:T(8,128)S(1)} %dynamic-slice_bitcast_fusion.2, pred[512,2048]{1,0:T(8,128)(4,1)S(1)} %broadcast_compare_fusion.5, pred[]{:T(512)S(6)} %compare.3, ...), kind=kOutput, calls=%fused_computation.23.clone.1 | convolution fusion | flops 832045056 | bytes 32911364 | tf_op jit(solution)/shard_map/while/body/eval_jaxpr/hqk,qhd->khd/dot_general | solution.py:163
  572.8 18.1 %multiply_reduce_fusion.3 = (f32[6,512]{1,0:T(8,128)S(1)}, f32[6,512,2048]{2,1,0:T(8,128)}) fusion(f32[6,512,2048]{2,1,0:T(8,128)} %fusion.140, f32[6,512]{1,0:T(8,128)S(1)} %dynamic-slice_bitcast_fusion.2, pred[512,2048]{1,0:T(8,128)(4,1)S(1)} %broadcast_compare_fusion.5, bf16[2048,6,64]{0,2,1:T(8,128)(2,1)} %get-tuple-element.508, ...), kind=kOutput, calls=%fused_computation.18.clone.1 | convolution fusion | flops 836760576 | bytes 53370884 | tf_op jit(solution)/shard_map/while/body/eval_jaxpr/qhd,khd->hqk/dot_general | solution.py:169
  590.9 21.3 %multiply_convert_fusion.3 = bf16[6,512,2048]{2,1,0:T(8,128)(2,1)} fusion(f32[6,512,2048]{2,1,0:T(8,128)} %get-tuple-element.443, f32[6,512,2048]{2,1,0:T(8,128)} %fusion.140, f32[6,512]{1,0:T(8,128)S(1)} %get-tuple-element.444, f32[6,512]{1,0:T(8,128)S(1)} %dynamic-slice_bitcast_fusion.2, pred[512,2048]{1,0:T(8,128)(4,1)S(1)} %broadcast_compare_fusion.5), kind=kLoop, calls=%fused_computation.17.clone.1 | loop fusion | flops 37748736 | bytes 63987712 | tf_op jit(solution)/shard_map/while/body/eval_jaxpr/convert_element_type | solution.py:173
  612.2 9.3 fusion.141
  621.4 9.6 bitcast_add_fusion.4
  631.7 11.0 fusion.140
  642.7 13.7 %bitcast_add_fusion.5 = f32[2048,6,64]{0,2,1:T(8,128)} fusion(f32[2048,6,64]{0,2,1:T(8,128)} %get-tuple-element.487, f32[6,512,2048]{2,1,0:T(8,128)} %fusion.140, f32[6,512]{1,0:T(8,128)S(1)} %dynamic-slice_bitcast_fusion.2, pred[512,2048]{1,0:T(8,128)(4,1)S(1)} %broadcast_compare_fusion.5, pred[]{:T(512)S(6)} %compare.3, ...), kind=kOutput, calls=%fused_computation.23.clone.1 | convolution fusion | flops 832045056 | bytes 32911364 | tf_op jit(solution)/shard_map/while/body/eval_jaxpr/hqk,qhd->khd/dot_general | solution.py:163
  656.4 18.1 %multiply_reduce_fusion.3 = (f32[6,512]{1,0:T(8,128)S(1)}, f32[6,512,2048]{2,1,0:T(8,128)}) fusion(f32[6,512,2048]{2,1,0:T(8,128)} %fusion.140, f32[6,512]{1,0:T(8,128)S(1)} %dynamic-slice_bitcast_fusion.2, pred[512,2048]{1,0:T(8,128)(4,1)S(1)} %broadcast_compare_fusion.5, bf16[2048,6,64]{0,2,1:T(8,128)(2,1)} %get-tuple-element.508, ...), kind=kOutput, calls=%fused_computation.18.clone.1 | convolution fusion | flops 836760576 | bytes 53370884 | tf_op jit(solution)/shard_map/while/body/eval_jaxpr/qhd,khd->hqk/dot_general | solution.py:169
  674.5 21.3 %multiply_convert_fusion.3 = bf16[6,512,2048]{2,1,0:T(8,128)(2,1)} fusion(f32[6,512,2048]{2,1,0:T(8,128)} %get-tuple-element.443, f32[6,512,2048]{2,1,0:T(8,128)} %fusion.140, f32[6,512]{1,0:T(8,128)S(1)} %get-tuple-element.444, f32[6,512]{1,0:T(8,128)S(1)} %dynamic-slice_bitcast_fusion.2, pred[512,2048]{1,0:T(8,128)(4,1)S(1)} %broadcast_compare_fusion.5), kind=kLoop, calls=%fused_computation.17.clone.1 | loop fusion | flops 37748736 | bytes 63987712 | tf_op jit(solution)/shard_map/while/body/eval_jaxpr/convert_element_type | solution.py:173
  695.8 9.3 fusion.141
  705.0 9.6 bitcast_add_fusion.4
  715.0 3.8 copy.52
  732.9 8.9 bitcast_convert_fusion
  741.9 9.8 fusion.81
  751.7 9.1 fusion.82
  764.5 5.8 fusion.66
  772.7 81.2 %all-reduce.1 = (f32[2,384]{1,0:T(2,128)}, f32[1536]{0:T(1024)}) all-reduce(f32[2,384]{1,0:T(2,128)S(1)} %pad_maximum_fusion.6, f32[1536]{0:T(1024)S(1)} %copy-done.38), channel_id=1, replica_groups=mesh['dp'=16,'mp'=2] {'dp'}, use_global_device_ids=true, to_apply=%region_38.39 | all-reduce | flops 2304 | bytes 18432 | tf_op jit(solution)/shard_map/psum | solution.py:234
  858.7 41.5 %all-reduce = (f32[2,768]{1,0:T(2,128)}, f32[4,768]{1,0:T(4,128)}) all-reduce(f32[2,768]{1,0:T(2,128)S(1)} %pad_maximum_fusion.5, f32[4,768]{1,0:T(4,128)S(1)} %pad_maximum_fusion.3), channel_id=1, replica_groups=mesh['dp'=16,'mp'=2] {'dp','mp'}, use_global_device_ids=true, to_apply=%region_29.30 | all-reduce | flops 4608 | bytes 36864 | tf_op jit(solution)/shard_map/psum | solution.py:220
  900.1 4.1 add_add_fusion.2
  904.2 267.0 %all-reduce.5.cloned.1.call-done = (f32[3,768,384]{1,2,0:T(8,128)}, f32[384,768]{1,0:T(8,128)}, f32[768,1536]{1,0:T(8,128)}, f32[1536,768]{1,0:T(8,128)}) async-done(((f32[3,768,384]{1,2,0:T(8,128)}, f32[384,768]{1,0:T(8,128)}, f32[768,1536]{1,0:T(8,128)}, f32[1536,768]{1,0:T(8,128)}), (f32[3,768,384]{1,2,0:T(8,128)}, f32[384,768]{1,0:T(8,128)}, f32[768,1536]{1,0:T(8,128)}, ...) | async-done | bytes 14155792 | tf_op jit(solution)/shard_map/psum | solution.py:234
  1171.3 5.2 copy.57
  1177.5 5.5 copy.92
  (237 shorter events, 87.9 us)
Async XLA Ops:
  7.2 275.3 %copy-start = (bf16[768,1536]{1,0:T(8,128)(2,1)S(1)}, bf16[768,1536]{1,0:T(8,128)(2,1)}, u32[]{:S(2)}) copy-start(bf16[768,1536]{1,0:T(8,128)(2,1)} %param.25) | copy-start | bytes 7077892
  7.2 4.6 copy-start.39
  7.2 5.2 copy-start.37
  7.2 22.6 %all-gather.5.cloned.1.call-start = ((), (), s32[]{:S(2)}) async-start(), calls=%async_computation.4 | async-start | bytes 4718592 | tf_op jit(solution)/shard_map/all_gather | solution.py:78
  7.3 5.8 copy-start.3
  9.1 3.9 copy-start.22
  9.1 5.8 copy-start.41
  9.1 6.3 copy-start.40
  11.8 1.3 copy-start.27
  14.8 211.6 %reduce-scatter.5.cloned.1.call-start = ((), (), s32[]{:S(2)}) async-start(), calls=%async_computation.5 | async-start | bytes 4718592 | tf_op jit(solution)/shard_map/reduce_scatter | solution.py:107
  61.6 12.1 %copy-start.7 = (bf16[2048,6,64]{0,2,1:T(8,128)(2,1)S(1)}, bf16[2048,6,64]{0,2,1:T(8,128)(2,1)}, u32[]{:S(2)}) copy-start(bf16[2048,6,64]{0,2,1:T(8,128)(2,1)} %get-tuple-element.470) | copy-start | bytes 4718596 | tf_op jit(solution)/shard_map/while
  61.6 12.1 %copy-start.13 = (bf16[4,512,6,64]{1,3,2,0:T(8,128)(2,1)S(1)}, bf16[4,512,6,64]{1,3,2,0:T(8,128)(2,1)}, u32[]{:S(2)}) copy-start(bf16[4,512,6,64]{1,3,2,0:T(8,128)(2,1)} %get-tuple-element.455) | copy-start | bytes 4718596 | tf_op jit(solution)/shard_map/while
  85.4 1.1 copy-start.14
  101.5 12.1 %copy-start.7 = (bf16[2048,6,64]{0,2,1:T(8,128)(2,1)S(1)}, bf16[2048,6,64]{0,2,1:T(8,128)(2,1)}, u32[]{:S(2)}) copy-start(bf16[2048,6,64]{0,2,1:T(8,128)(2,1)} %get-tuple-element.470) | copy-start | bytes 4718596 | tf_op jit(solution)/shard_map/while
  101.5 12.1 %copy-start.13 = (bf16[4,512,6,64]{1,3,2,0:T(8,128)(2,1)S(1)}, bf16[4,512,6,64]{1,3,2,0:T(8,128)(2,1)}, u32[]{:S(2)}) copy-start(bf16[4,512,6,64]{1,3,2,0:T(8,128)(2,1)} %get-tuple-element.455) | copy-start | bytes 4718596 | tf_op jit(solution)/shard_map/while
  125.2 1.1 copy-start.14
  141.3 12.1 %copy-start.7 = (bf16[2048,6,64]{0,2,1:T(8,128)(2,1)S(1)}, bf16[2048,6,64]{0,2,1:T(8,128)(2,1)}, u32[]{:S(2)}) copy-start(bf16[2048,6,64]{0,2,1:T(8,128)(2,1)} %get-tuple-element.470) | copy-start | bytes 4718596 | tf_op jit(solution)/shard_map/while
  141.3 12.1 %copy-start.13 = (bf16[4,512,6,64]{1,3,2,0:T(8,128)(2,1)S(1)}, bf16[4,512,6,64]{1,3,2,0:T(8,128)(2,1)}, u32[]{:S(2)}) copy-start(bf16[4,512,6,64]{1,3,2,0:T(8,128)(2,1)} %get-tuple-element.455) | copy-start | bytes 4718596 | tf_op jit(solution)/shard_map/while
  165.1 1.1 copy-start.14
  181.2 12.1 %copy-start.7 = (bf16[2048,6,64]{0,2,1:T(8,128)(2,1)S(1)}, bf16[2048,6,64]{0,2,1:T(8,128)(2,1)}, u32[]{:S(2)}) copy-start(bf16[2048,6,64]{0,2,1:T(8,128)(2,1)} %get-tuple-element.470) | copy-start | bytes 4718596 | tf_op jit(solution)/shard_map/while
  181.2 12.1 %copy-start.13 = (bf16[4,512,6,64]{1,3,2,0:T(8,128)(2,1)S(1)}, bf16[4,512,6,64]{1,3,2,0:T(8,128)(2,1)}, u32[]{:S(2)}) copy-start(bf16[4,512,6,64]{1,3,2,0:T(8,128)(2,1)} %get-tuple-element.455) | copy-start | bytes 4718596 | tf_op jit(solution)/shard_map/while
  205.0 1.1 copy-start.14
  206.3 4.3 copy-start.47
  209.4 1.2 copy-start.15
  214.1 12.3 %copy-start.21 = (f32[768]{0:T(1024)S(1)}, f32[768]{0:T(1024)}, u32[]{:S(2)}) copy-start(f32[768]{0:T(1024)} %get-tuple-element.249) | copy-start | bytes 9220
  214.2 68.3 %all-gather.7.cloned.1.call-start = ((), (), s32[]{:S(2)}) async-start(), calls=%async_computation.6 | async-start | bytes 4718592 | tf_op jit(solution)/shard_map/all_gather | solution.py:115
  226.4 2.6 copy-start.4
  226.4 2.8 copy-start.8
  226.4 3.7 copy-start.26
  226.4 3.7 copy-start.34
  230.1 2.8 copy-start.42
  232.2 50.3 %copy-start.48 = (f32[1536]{0:T(1024)S(1)}, f32[1536]{0:T(1024)}, u32[]{:S(2)}) copy-start(f32[1536]{0:T(1024)} %param.26) | copy-start | bytes 18436
  232.2 64.0 %all-gather.9.cloned.1.call-start = ((), (), s32[]{:S(2)}) async-start(), calls=%async_computation.8 | async-start | bytes 4718592 | tf_op jit(solution)/shard_map/all_gather | solution.py:128
  282.4 54.2 %reduce-scatter.9.cloned.1.call-start = ((), (), s32[]{:S(2)}) async-start(), calls=%async_computation.9 | async-start | bytes 4718592 | tf_op jit(solution)/shard_map/reduce_scatter | solution.py:139
  315.6 2.6 copy-start.49
  324.6 1.7 copy-start.46
  324.7 21.7 %reduce-scatter.7.cloned.1.call-start = ((), (), s32[]{:S(2)}) async-start(), calls=%async_computation.7 | async-start | bytes 4718592 | tf_op jit(solution)/shard_map/reduce_scatter | solution.py:120
  335.9 1.4 copy-start.5
  336.0 32.4 %all-gather.11.cloned.1.call-start = ((), (), s32[]{:S(2)}) async-start(), calls=%async_computation.10 | async-start | bytes 4718592 | tf_op jit(solution)/shard_map/all_gather | solution.py:149
  337.4 3.9 copy-start.12
  341.2 5.1 copy-start.31
  351.9 1.7 copy-start.9
  354.9 499.0 %reduce-scatter.11.cloned.1.call-start = ((), (), s32[]{:S(2)}) async-start(), calls=%async_computation.11 | async-start | bytes 4718592 | tf_op jit(solution)/shard_map/reduce_scatter | solution.py:210
  377.3 4.4 copy-start.2
  721.6 5.0 copy-start.10
  741.8 429.4 %all-reduce.5.cloned.1.call-start = ((), (), s32[]{:S(2)}) async-start(), calls=%async_computation.12 | async-start | bytes 28311552 | tf_op jit(solution)/shard_map/psum | solution.py:234
  741.9 9.8 copy-start.44
  751.7 9.1 copy-start.16
  751.7 9.1 copy-start.45
  760.7 2.4 copy-start.17
  760.8 2.4 copy-start.18
  760.8 2.4 copy-start.19
  760.8 3.7 copy-start.43
  770.3 2.5 copy-start.38
  770.3 83.7 %copy-start.6 = (bf16[1024,768]{1,0:T(8,128)(2,1)S(1)}, bf16[1024,768]{1,0:T(8,128)(2,1)}, u32[]{:S(2)}) copy-start(bf16[1024,768]{1,0:T(8,128)(2,1)} %param.16) | copy-start | bytes 4718596
  770.3 83.7 %copy-start.23 = (f32[1024]{0:T(1024)S(1)}, f32[1024]{0:T(1024)}, u32[]{:S(2)}) copy-start(f32[1024]{0:T(1024)} %copy-done.22) | copy-start | bytes 12292
  770.3 83.6 %copy-start.25 = (f32[768]{0:T(1024)S(1)}, f32[768]{0:T(1024)}, u32[]{:S(2)}) copy-start(f32[768]{0:T(1024)} %copy-done.24) | copy-start | bytes 9220
  770.3 86.3 %copy-start.30 = (f32[1024]{0:T(1024)S(1)}, f32[1024]{0:T(1024)}, u32[]{:S(2)}) copy-start(f32[1024]{0:T(1024)} %copy-done.29) | copy-start | bytes 12292
  770.3 86.3 %copy-start.28 = (f32[1024]{0:T(1024)S(1)}, f32[1024]{0:T(1024)}, u32[]{:S(2)}) copy-start(f32[1024]{0:T(1024)} %copy-done.27) | copy-start | bytes 12292
  854.0 2.7 copy-start.11
  1171.3 5.3 copy-start.20
  1176.5 6.5 slice-start
  1177.5 5.5 slice-start.1
  1177.5 7.7 copy-start.1
  (6 other events, 4.0 us)
Sparse Core Ops, SparseCore 0:
  15.0 14.8 all-gather.4
  214.3 12.0 reduce-scatter.4
  232.3 13.3 all-gather.6
  282.5 7.9 all-gather.8
  324.8 6.7 reduce-scatter.8
  336.1 10.2 reduce-scatter.6
  355.1 13.2 all-gather.10
  742.0 12.0 reduce-scatter.10
  770.5 400.7 all-reduce.4
where the time goes:
time: 1200 us; the launch traced here: 1190 us
  matrix products  448 us (37%)
  waiting for transfers between devices  308 us (26%)
  other arithmetic  188 us (16%)
  blocking collectives  165 us (14%)
  local copies, waits for them, and re-layouts  65.3 us (5%)
  between operations  15.9 us (1%)
    psum x1, waiting for transfers between devices, local(): lax.psum((grad_qkv, grad_qv_bias, grad_out, grad_fc1, grad_bfc1, grad_fc2...  267 us
    dot_general x8, matrix products, score_block(): jnp.einsum('qhd,khd->hqk', query_block, keys_all, preferred_element_type=...  101 us
    convert_element_type x4, other arithmetic, backward_block(): grad_scores = grad_scores.astype(jnp.bfloat16)  85.1 us
    psum x1, blocking collectives, local(): lax.psum((grad_qkv, grad_qv_bias, grad_out, grad_fc1, grad_bfc1, grad_fc2...  81.2 us
    dot_general x4, matrix products, backward_block(): jnp.einsum('qhd,khd->hqk', grad_block, values_all, preferred_element_type...  72.3 us
    dot_general x4, matrix products, backward_block(): jnp.einsum('hqk,qhd->khd', probs.astype(jnp.bfloat16), grad_block, prefer...  53.8 us
    reduce_sum x4, other arithmetic, forward_block(): total = jnp.sum(exponent, axis=-1, keepdims=True)  48.4 us
    dot_general x4, matrix products, forward_block(): jnp.einsum('hqk,khd->qhd', weights, values_all, preferred_element_type=jn...  46.6 us
  transfers between devices with their start and end apart: 9, of which 5 were waited for; matrix products, arithmetic and copies ran while one was open for 6% of the time, Pallas kernels for 0%

commit v1 on v0

--- a/solution.py
+++ b/solution.py
@@ -61,7 +61,7 @@
     segment, row_length = image_rows(image_lengths[0], row_count)
     images = jnp.sum((image_lengths[0] > 0).astype(jnp.float32))
     member = (group_of_block[0] == jnp.arange(GROUPS, dtype=jnp.int32)).astype(jnp.float32)
-    group_images = lax.psum(member * images, "dp")
+    group_images = jnp.sum(lax.all_gather(member * images, "dp"), axis=0)
     group_roots = jnp.sqrt(group_images)
     factor = jnp.sum(group_images) / (group_roots * jnp.sum(group_roots))
     block_factor = jnp.sum(member * factor)

time: 1200 us -> 1200 us (level)
    psum x1 -> x0, blocking collectives: 41.9 us -> none  [local(): group_images = lax.psum(member * images, 'dp')]
    all_gather x0 -> x1, blocking collectives: none -> 40.6 us  [local(): group_images = jnp.sum(lax.all_gather(member * images, 'dp'), axis=0)]
where the time goes in v1:
time: 1200 us; the launch traced here: 1190 us
  matrix products  448 us (37%)
  waiting for transfers between devices  308 us (26%)
  other arithmetic  189 us (16%)
  blocking collectives  163 us (14%)
  local copies, waits for them, and re-layouts  65.3 us (5%)
  between operations  15.9 us (1%)
    psum x1, waiting for transfers between devices, local(): lax.psum((grad_qkv, grad_qv_bias, grad_out, grad_fc1, grad_bfc1, grad_fc2...  267 us
    dot_general x8, matrix products, score_block(): jnp.einsum('qhd,khd->hqk', query_block, keys_all, preferred_element_type=...  101 us
    convert_element_type x4, other arithmetic, backward_block(): grad_scores = grad_scores.astype(jnp.bfloat16)  85.1 us
    psum x1, blocking collectives, local(): lax.psum((grad_qkv, grad_qv_bias, grad_out, grad_fc1, grad_bfc1, grad_fc2...  81.2 us
    dot_general x4, matrix products, backward_block(): jnp.einsum('qhd,khd->hqk', grad_block, values_all, preferred_element_type...  72.3 us
    dot_general x4, matrix products, backward_block(): jnp.einsum('hqk,qhd->khd', probs.astype(jnp.bfloat16), grad_block, prefer...  53.8 us
    reduce_sum x4, other arithmetic, forward_block(): total = jnp.sum(exponent, axis=-1, keepdims=True)  48.4 us
    dot_general x4, matrix products, forward_block(): jnp.einsum('hqk,khd->qhd', weights, values_all, preferred_element_type=jn...  46.6 us
  transfers between devices with their start and end apart: 9, of which 5 were waited for; matrix products, arithmetic and copies ran while one was open for 6% of the time, Pallas kernels for 0%

profile of v1, /device:TPU:0, one launch (start us, length us, event | category | flops | bytes accessed | tf_op | source)
XLA Modules:
  0.0 1191.3 jit_solution(15593499263766875377)
XLA Ops:
  15.5 14.2 %all-gather.6.cloned.1.call-done = bf16[2048,768]{1,0:T(8,128)(2,1)} async-done(((bf16[1024,768]{1,0:T(8,128)(2,1)}), bf16[2048,768]{1,0:T(8,128)(2,1)}) %all-gather.6.cloned.1.call-update) | async-done | bytes 3145744 | tf_op jit(solution)/shard_map/all_gather | solution.py:78
  29.8 6.3 fusion.45
  38.4 4.0 reshape_squeeze.3
  46.6 159.6 %while.27 = (s32[]{:T(128)}, bf16[4,512,6,64]{1,3,2,0:T(8,128)(2,1)}, f32[4,6,512]{2,1,0:T(8,128)S(1)}, s32[4,512]{1,0:T(4,128)S(1)}, s32[2048]{0:T(1024)S(1)}, ...) while((s32[]{:T(128)}, ...), condition=%wide.region_7.8_spmd, body=%wide.region_4.7_spmd.sunk | while | flops 1687155712 | bytes 103024832 | solution.py:104
  47.3 14.3 %fusion.129 = (f32[6,512]{1,0:T(8,128)S(1)}, f32[6,512,2048]{2,1,0:T(8,128)}) fusion(pred[512,2048]{1,0:T(8,128)(4,1)S(1)} %broadcast_compare_fusion.4, bf16[2048,6,64]{0,2,1:T(8,128)(2,1)} %get-tuple-element.500, bf16[4,512,6,64]{1,3,2,0:T(8,128)(2,1)} %get-tuple-element.499, s32[]{:T(128)S(6)} %copy.80), kind=kOutput, calls=%fused_computation.3.clone.1 | convolution fusion | flops 824177664 | bytes 28192772 | tf_op jit(solution)/shard_map/while/body/eval_jaxpr/qhd,khd->hqk/dot_general | solution.py:38
  61.6 12.1 %fusion.130 = f32[6,512]{1,0:T(8,128)S(1)} fusion(f32[6,512,2048]{2,1,0:T(8,128)} %get-tuple-element.461, f32[6,512]{1,0:T(8,128)S(1)} %get-tuple-element.462, pred[512,2048]{1,0:T(8,128)(4,1)S(1)} %broadcast_compare_fusion.4), kind=kLoop, calls=%fused_computation.4.clone.1 | loop fusion | flops 25162752 | bytes 26238976 | tf_op jit(solution)/shard_map/while/body/eval_jaxpr/reduce_sum | solution.py:97
  73.7 11.6 fusion.131
  87.2 14.3 %fusion.129 = (f32[6,512]{1,0:T(8,128)S(1)}, f32[6,512,2048]{2,1,0:T(8,128)}) fusion(pred[512,2048]{1,0:T(8,128)(4,1)S(1)} %broadcast_compare_fusion.4, bf16[2048,6,64]{0,2,1:T(8,128)(2,1)} %get-tuple-element.500, bf16[4,512,6,64]{1,3,2,0:T(8,128)(2,1)} %get-tuple-element.499, s32[]{:T(128)S(6)} %copy.80), kind=kOutput, calls=%fused_computation.3.clone.1 | convolution fusion | flops 824177664 | bytes 28192772 | tf_op jit(solution)/shard_map/while/body/eval_jaxpr/qhd,khd->hqk/dot_general | solution.py:38
  101.4 12.1 %fusion.130 = f32[6,512]{1,0:T(8,128)S(1)} fusion(f32[6,512,2048]{2,1,0:T(8,128)} %get-tuple-element.461, f32[6,512]{1,0:T(8,128)S(1)} %get-tuple-element.462, pred[512,2048]{1,0:T(8,128)(4,1)S(1)} %broadcast_compare_fusion.4), kind=kLoop, calls=%fused_computation.4.clone.1 | loop fusion | flops 25162752 | bytes 26238976 | tf_op jit(solution)/shard_map/while/body/eval_jaxpr/reduce_sum | solution.py:97
  113.6 11.6 fusion.131
  127.0 14.3 %fusion.129 = (f32[6,512]{1,0:T(8,128)S(1)}, f32[6,512,2048]{2,1,0:T(8,128)}) fusion(pred[512,2048]{1,0:T(8,128)(4,1)S(1)} %broadcast_compare_fusion.4, bf16[2048,6,64]{0,2,1:T(8,128)(2,1)} %get-tuple-element.500, bf16[4,512,6,64]{1,3,2,0:T(8,128)(2,1)} %get-tuple-element.499, s32[]{:T(128)S(6)} %copy.80), kind=kOutput, calls=%fused_computation.3.clone.1 | convolution fusion | flops 824177664 | bytes 28192772 | tf_op jit(solution)/shard_map/while/body/eval_jaxpr/qhd,khd->hqk/dot_general | solution.py:38
  141.3 12.1 %fusion.130 = f32[6,512]{1,0:T(8,128)S(1)} fusion(f32[6,512,2048]{2,1,0:T(8,128)} %get-tuple-element.461, f32[6,512]{1,0:T(8,128)S(1)} %get-tuple-element.462, pred[512,2048]{1,0:T(8,128)(4,1)S(1)} %broadcast_compare_fusion.4), kind=kLoop, calls=%fused_computation.4.clone.1 | loop fusion | flops 25162752 | bytes 26238976 | tf_op jit(solution)/shard_map/while/body/eval_jaxpr/reduce_sum | solution.py:97
  153.4 11.6 fusion.131
  166.9 14.3 %fusion.129 = (f32[6,512]{1,0:T(8,128)S(1)}, f32[6,512,2048]{2,1,0:T(8,128)}) fusion(pred[512,2048]{1,0:T(8,128)(4,1)S(1)} %broadcast_compare_fusion.4, bf16[2048,6,64]{0,2,1:T(8,128)(2,1)} %get-tuple-element.500, bf16[4,512,6,64]{1,3,2,0:T(8,128)(2,1)} %get-tuple-element.499, s32[]{:T(128)S(6)} %copy.80), kind=kOutput, calls=%fused_computation.3.clone.1 | convolution fusion | flops 824177664 | bytes 28192772 | tf_op jit(solution)/shard_map/while/body/eval_jaxpr/qhd,khd->hqk/dot_general | solution.py:38
  181.2 12.1 %fusion.130 = f32[6,512]{1,0:T(8,128)S(1)} fusion(f32[6,512,2048]{2,1,0:T(8,128)} %get-tuple-element.461, f32[6,512]{1,0:T(8,128)S(1)} %get-tuple-element.462, pred[512,2048]{1,0:T(8,128)(4,1)S(1)} %broadcast_compare_fusion.4), kind=kLoop, calls=%fused_computation.4.clone.1 | loop fusion | flops 25162752 | bytes 26238976 | tf_op jit(solution)/shard_map/while/body/eval_jaxpr/reduce_sum | solution.py:97
  193.3 11.6 fusion.131
  210.6 3.5 convolution_convert_fusion
  214.2 12.2 %reduce-scatter.5.cloned.1.call-done = bf16[1024,768]{1,0:T(8,128)(2,1)} async-done(((bf16[2048,768]{1,0:T(8,128)(2,1)}), bf16[1024,768]{1,0:T(8,128)(2,1)}) %reduce-scatter.5.cloned.1.call-update) | async-done | bytes 1572880 | tf_op jit(solution)/shard_map/reduce_scatter | solution.py:107
  234.1 40.6 %all-gather = f32[16,1,3]{2,1,0:T(1,128)S(1)} all-gather(f32[1,1,3]{2,1,0:T(1,128)S(1)} %fusion.71), channel_id=1, replica_groups=mesh['dp'=16,'mp'=2] {'dp'}, dimensions={0}, use_global_device_ids=true | all-gather | bytes 204 | tf_op jit(solution)/shard_map/all_gather | solution.py:64
  281.7 13.7 %multiply_convert_fusion.1 = (bf16[2048,1536]{1,0:T(8,128)(2,1)}, f32[2048,1536]{1,0:T(8,128)}) fusion(f32[1536]{0:T(1024)S(1)} %copy-done.48, bf16[2048,768]{1,0:T(8,128)(2,1)} %all-gather.8.cloned.1.call-done, bf16[768,1536]{1,0:T(8,128)(2,1)S(1)} %copy-done), kind=kOutput, calls=%fused_computation.58 | convolution fusion | flops 4863295488 | bytes 24385536 | tf_op jit(solution)/shard_map/dot_general | solution.py:116
  295.4 19.5 %convert_reduce_fusion = (f32[1536]{0:T(1024)}, bf16[2048,1536]{1,0:T(8,128)(2,1)S(1)}) fusion(bf16[2048,768]{1,0:T(8,128)(2,1)} %all-gather.10.cloned.1.call-done, bf16[1536,768]{1,0:T(8,128)(2,1)} %param.27, f32[2048,1536]{1,0:T(8,128)} %get-tuple-element.347, f32[1536]{0:T(1024)S(1)} %copy-done.48), kind=kOutput, calls=%fused_computation.57 | convolution fusion | flops 4916771328 | bytes 24391680 | tf_op jit(solution)/shard_map/rd,fd->rf/dot_general | solution.py:132
  317.5 6.4 convolution_convert_fusion.1
  325.6 9.7 convolution_convert_fusion.2
  336.6 3.9 convert_reduce_fusion.2
  340.5 4.2 fusion.56
  345.6 5.6 fusion.78
  354.3 13.4 %all-gather.12.cloned.1.call-done = bf16[2048,768]{1,0:T(8,128)(2,1)} async-done(((bf16[1024,768]{1,0:T(8,128)(2,1)}), bf16[2048,768]{1,0:T(8,128)(2,1)}) %all-gather.12.cloned.1.call-update) | async-done | bytes 3145744 | tf_op jit(solution)/shard_map/all_gather | solution.py:149
  367.6 4.9 convolution_convert_fusion.3
  381.0 333.3 %while.28 = (s32[]{:T(128)}, f32[2048,6,64]{0,2,1:T(8,128)}, f32[2048,6,64]{0,2,1:T(8,128)}, bf16[4,512,6,64]{1,3,2,0:T(8,128)(2,1)}, bf16[4,512,6,64]{1,3,2,0:T...) while((s32[]{:T(128)}, f32[2048,6,64]{0,2,1:T(8,128)}, ...), condition=%wide.region_23.24_spmd.clone, body=%wide.region_21.23_spmd.clone.sunk | while | flops 4126077952 | bytes 212699312 | solution.py:188
  381.9 11.0 fusion.141
  392.9 12.8 %bitcast_add_fusion.5 = f32[2048,6,64]{0,2,1:T(8,128)} fusion(f32[2048,6,64]{0,2,1:T(8,128)} %get-tuple-element.518, f32[6,512,2048]{2,1,0:T(8,128)} %fusion.141, f32[6,512]{1,0:T(8,128)S(1)} %dynamic-slice_bitcast_fusion.2, pred[512,2048]{1,0:T(8,128)(4,1)S(1)} %broadcast_compare_fusion.5, pred[]{:T(512)S(6)} %compare.3, ...), kind=kOutput, calls=%fused_computation.23.clone.1 | convolution fusion | flops 832045056 | bytes 32911364 | tf_op jit(solution)/shard_map/while/body/eval_jaxpr/hqk,qhd->khd/dot_general | solution.py:163
  405.8 18.1 %multiply_reduce_fusion.3 = (f32[6,512]{1,0:T(8,128)S(1)}, f32[6,512,2048]{2,1,0:T(8,128)}) fusion(f32[6,512,2048]{2,1,0:T(8,128)} %fusion.141, f32[6,512]{1,0:T(8,128)S(1)} %dynamic-slice_bitcast_fusion.2, pred[512,2048]{1,0:T(8,128)(4,1)S(1)} %broadcast_compare_fusion.5, bf16[2048,6,64]{0,2,1:T(8,128)(2,1)} %get-tuple-element.539, ...), kind=kOutput, calls=%fused_computation.18.clone.1 | convolution fusion | flops 836760576 | bytes 53370884 | tf_op jit(solution)/shard_map/while/body/eval_jaxpr/qhd,khd->hqk/dot_general | solution.py:169
  423.8 21.3 %multiply_convert_fusion.3 = bf16[6,512,2048]{2,1,0:T(8,128)(2,1)} fusion(f32[6,512,2048]{2,1,0:T(8,128)} %get-tuple-element.474, f32[6,512,2048]{2,1,0:T(8,128)} %fusion.141, f32[6,512]{1,0:T(8,128)S(1)} %get-tuple-element.475, f32[6,512]{1,0:T(8,128)S(1)} %dynamic-slice_bitcast_fusion.2, pred[512,2048]{1,0:T(8,128)(4,1)S(1)} %broadcast_compare_fusion.5), kind=kLoop, calls=%fused_computation.17.clone.1 | loop fusion | flops 37748736 | bytes 63987712 | tf_op jit(solution)/shard_map/while/body/eval_jaxpr/convert_element_type | solution.py:173
  445.1 9.3 fusion.142
  454.4 8.7 bitcast_add_fusion.4
  463.8 11.0 fusion.141
  474.8 13.7 %bitcast_add_fusion.5 = f32[2048,6,64]{0,2,1:T(8,128)} fusion(f32[2048,6,64]{0,2,1:T(8,128)} %get-tuple-element.518, f32[6,512,2048]{2,1,0:T(8,128)} %fusion.141, f32[6,512]{1,0:T(8,128)S(1)} %dynamic-slice_bitcast_fusion.2, pred[512,2048]{1,0:T(8,128)(4,1)S(1)} %broadcast_compare_fusion.5, pred[]{:T(512)S(6)} %compare.3, ...), kind=kOutput, calls=%fused_computation.23.clone.1 | convolution fusion | flops 832045056 | bytes 32911364 | tf_op jit(solution)/shard_map/while/body/eval_jaxpr/hqk,qhd->khd/dot_general | solution.py:163
  488.5 18.1 %multiply_reduce_fusion.3 = (f32[6,512]{1,0:T(8,128)S(1)}, f32[6,512,2048]{2,1,0:T(8,128)}) fusion(f32[6,512,2048]{2,1,0:T(8,128)} %fusion.141, f32[6,512]{1,0:T(8,128)S(1)} %dynamic-slice_bitcast_fusion.2, pred[512,2048]{1,0:T(8,128)(4,1)S(1)} %broadcast_compare_fusion.5, bf16[2048,6,64]{0,2,1:T(8,128)(2,1)} %get-tuple-element.539, ...), kind=kOutput, calls=%fused_computation.18.clone.1 | convolution fusion | flops 836760576 | bytes 53370884 | tf_op jit(solution)/shard_map/while/body/eval_jaxpr/qhd,khd->hqk/dot_general | solution.py:169
  506.6 21.3 %multiply_convert_fusion.3 = bf16[6,512,2048]{2,1,0:T(8,128)(2,1)} fusion(f32[6,512,2048]{2,1,0:T(8,128)} %get-tuple-element.474, f32[6,512,2048]{2,1,0:T(8,128)} %fusion.141, f32[6,512]{1,0:T(8,128)S(1)} %get-tuple-element.475, f32[6,512]{1,0:T(8,128)S(1)} %dynamic-slice_bitcast_fusion.2, pred[512,2048]{1,0:T(8,128)(4,1)S(1)} %broadcast_compare_fusion.5), kind=kLoop, calls=%fused_computation.17.clone.1 | loop fusion | flops 37748736 | bytes 63987712 | tf_op jit(solution)/shard_map/while/body/eval_jaxpr/convert_element_type | solution.py:173
  527.9 9.3 fusion.142
  537.1 9.6 bitcast_add_fusion.4
  547.4 11.0 fusion.141
  558.4 13.7 %bitcast_add_fusion.5 = f32[2048,6,64]{0,2,1:T(8,128)} fusion(f32[2048,6,64]{0,2,1:T(8,128)} %get-tuple-element.518, f32[6,512,2048]{2,1,0:T(8,128)} %fusion.141, f32[6,512]{1,0:T(8,128)S(1)} %dynamic-slice_bitcast_fusion.2, pred[512,2048]{1,0:T(8,128)(4,1)S(1)} %broadcast_compare_fusion.5, pred[]{:T(512)S(6)} %compare.3, ...), kind=kOutput, calls=%fused_computation.23.clone.1 | convolution fusion | flops 832045056 | bytes 32911364 | tf_op jit(solution)/shard_map/while/body/eval_jaxpr/hqk,qhd->khd/dot_general | solution.py:163
  572.1 18.1 %multiply_reduce_fusion.3 = (f32[6,512]{1,0:T(8,128)S(1)}, f32[6,512,2048]{2,1,0:T(8,128)}) fusion(f32[6,512,2048]{2,1,0:T(8,128)} %fusion.141, f32[6,512]{1,0:T(8,128)S(1)} %dynamic-slice_bitcast_fusion.2, pred[512,2048]{1,0:T(8,128)(4,1)S(1)} %broadcast_compare_fusion.5, bf16[2048,6,64]{0,2,1:T(8,128)(2,1)} %get-tuple-element.539, ...), kind=kOutput, calls=%fused_computation.18.clone.1 | convolution fusion | flops 836760576 | bytes 53370884 | tf_op jit(solution)/shard_map/while/body/eval_jaxpr/qhd,khd->hqk/dot_general | solution.py:169
  590.2 21.3 %multiply_convert_fusion.3 = bf16[6,512,2048]{2,1,0:T(8,128)(2,1)} fusion(f32[6,512,2048]{2,1,0:T(8,128)} %get-tuple-element.474, f32[6,512,2048]{2,1,0:T(8,128)} %fusion.141, f32[6,512]{1,0:T(8,128)S(1)} %get-tuple-element.475, f32[6,512]{1,0:T(8,128)S(1)} %dynamic-slice_bitcast_fusion.2, pred[512,2048]{1,0:T(8,128)(4,1)S(1)} %broadcast_compare_fusion.5), kind=kLoop, calls=%fused_computation.17.clone.1 | loop fusion | flops 37748736 | bytes 63987712 | tf_op jit(solution)/shard_map/while/body/eval_jaxpr/convert_element_type | solution.py:173
  611.4 9.3 fusion.142
  620.7 9.6 bitcast_add_fusion.4
  631.0 11.0 fusion.141
  642.0 13.7 %bitcast_add_fusion.5 = f32[2048,6,64]{0,2,1:T(8,128)} fusion(f32[2048,6,64]{0,2,1:T(8,128)} %get-tuple-element.518, f32[6,512,2048]{2,1,0:T(8,128)} %fusion.141, f32[6,512]{1,0:T(8,128)S(1)} %dynamic-slice_bitcast_fusion.2, pred[512,2048]{1,0:T(8,128)(4,1)S(1)} %broadcast_compare_fusion.5, pred[]{:T(512)S(6)} %compare.3, ...), kind=kOutput, calls=%fused_computation.23.clone.1 | convolution fusion | flops 832045056 | bytes 32911364 | tf_op jit(solution)/shard_map/while/body/eval_jaxpr/hqk,qhd->khd/dot_general | solution.py:163
  655.7 18.1 %multiply_reduce_fusion.3 = (f32[6,512]{1,0:T(8,128)S(1)}, f32[6,512,2048]{2,1,0:T(8,128)}) fusion(f32[6,512,2048]{2,1,0:T(8,128)} %fusion.141, f32[6,512]{1,0:T(8,128)S(1)} %dynamic-slice_bitcast_fusion.2, pred[512,2048]{1,0:T(8,128)(4,1)S(1)} %broadcast_compare_fusion.5, bf16[2048,6,64]{0,2,1:T(8,128)(2,1)} %get-tuple-element.539, ...), kind=kOutput, calls=%fused_computation.18.clone.1 | convolution fusion | flops 836760576 | bytes 53370884 | tf_op jit(solution)/shard_map/while/body/eval_jaxpr/qhd,khd->hqk/dot_general | solution.py:169
  673.8 21.3 %multiply_convert_fusion.3 = bf16[6,512,2048]{2,1,0:T(8,128)(2,1)} fusion(f32[6,512,2048]{2,1,0:T(8,128)} %get-tuple-element.474, f32[6,512,2048]{2,1,0:T(8,128)} %fusion.141, f32[6,512]{1,0:T(8,128)S(1)} %get-tuple-element.475, f32[6,512]{1,0:T(8,128)S(1)} %dynamic-slice_bitcast_fusion.2, pred[512,2048]{1,0:T(8,128)(4,1)S(1)} %broadcast_compare_fusion.5), kind=kLoop, calls=%fused_computation.17.clone.1 | loop fusion | flops 37748736 | bytes 63987712 | tf_op jit(solution)/shard_map/while/body/eval_jaxpr/convert_element_type | solution.py:173
  695.0 9.3 fusion.142
  704.3 9.6 bitcast_add_fusion.4
  714.3 3.8 copy.65
  732.2 8.9 bitcast_convert_fusion
  741.2 9.8 fusion.82
  751.0 9.1 fusion.83
  763.8 5.8 fusion.66
  772.0 81.2 %all-reduce.1 = (f32[2,384]{1,0:T(2,128)}, f32[1536]{0:T(1024)}) all-reduce(f32[2,384]{1,0:T(2,128)S(1)} %pad_maximum_fusion.6, f32[1536]{0:T(1024)S(1)} %copy-done.38), channel_id=1, replica_groups=mesh['dp'=16,'mp'=2] {'dp'}, use_global_device_ids=true, to_apply=%region_38.39 | all-reduce | flops 2304 | bytes 18432 | tf_op jit(solution)/shard_map/psum | solution.py:234
  858.0 41.5 %all-reduce = (f32[2,768]{1,0:T(2,128)}, f32[4,768]{1,0:T(4,128)}) all-reduce(f32[2,768]{1,0:T(2,128)S(1)} %pad_maximum_fusion.5, f32[4,768]{1,0:T(4,128)S(1)} %pad_maximum_fusion.3), channel_id=1, replica_groups=mesh['dp'=16,'mp'=2] {'dp','mp'}, use_global_device_ids=true, to_apply=%region_29.30 | all-reduce | flops 4608 | bytes 36864 | tf_op jit(solution)/shard_map/psum | solution.py:220
  899.4 4.1 add_add_fusion.2
  903.5 267.0 %all-reduce.5.cloned.1.call-done = (f32[3,768,384]{1,2,0:T(8,128)}, f32[384,768]{1,0:T(8,128)}, f32[768,1536]{1,0:T(8,128)}, f32[1536,768]{1,0:T(8,128)}) async-done(((f32[3,768,384]{1,2,0:T(8,128)}, f32[384,768]{1,0:T(8,128)}, f32[768,1536]{1,0:T(8,128)}, f32[1536,768]{1,0:T(8,128)}), (f32[3,768,384]{1,2,0:T(8,128)}, f32[384,768]{1,0:T(8,128)}, f32[768,1536]{1,0:T(8,128)}, ...) | async-done | bytes 14155792 | tf_op jit(solution)/shard_map/psum | solution.py:234
  1170.5 5.2 copy.70
  1176.8 5.5 copy.105
  (237 shorter events, 88.4 us)
Async XLA Ops:
  7.2 274.5 %copy-start = (bf16[768,1536]{1,0:T(8,128)(2,1)S(1)}, bf16[768,1536]{1,0:T(8,128)(2,1)}, u32[]{:S(2)}) copy-start(bf16[768,1536]{1,0:T(8,128)(2,1)} %param.25) | copy-start | bytes 7077892
  7.2 4.6 copy-start.37
  7.2 4.6 copy-start.39
  7.2 22.6 %all-gather.6.cloned.1.call-start = ((), (), s32[]{:S(2)}) async-start(), calls=%async_computation.4 | async-start | bytes 4718592 | tf_op jit(solution)/shard_map/all_gather | solution.py:78
  7.3 5.7 copy-start.3
  9.1 3.3 copy-start.22
  9.1 5.7 copy-start.41
  9.1 6.3 copy-start.40
  14.8 211.6 %reduce-scatter.5.cloned.1.call-start = ((), (), s32[]{:S(2)}) async-start(), calls=%async_computation.5 | async-start | bytes 4718592 | tf_op jit(solution)/shard_map/reduce_scatter | solution.py:107
  61.6 12.1 %copy-start.7 = (bf16[2048,6,64]{0,2,1:T(8,128)(2,1)S(1)}, bf16[2048,6,64]{0,2,1:T(8,128)(2,1)}, u32[]{:S(2)}) copy-start(bf16[2048,6,64]{0,2,1:T(8,128)(2,1)} %get-tuple-element.501) | copy-start | bytes 4718596 | tf_op jit(solution)/shard_map/while
  61.6 12.1 %copy-start.13 = (bf16[4,512,6,64]{1,3,2,0:T(8,128)(2,1)S(1)}, bf16[4,512,6,64]{1,3,2,0:T(8,128)(2,1)}, u32[]{:S(2)}) copy-start(bf16[4,512,6,64]{1,3,2,0:T(8,128)(2,1)} %get-tuple-element.486) | copy-start | bytes 4718596 | tf_op jit(solution)/shard_map/while
  85.4 1.1 copy-start.14
  101.4 12.1 %copy-start.7 = (bf16[2048,6,64]{0,2,1:T(8,128)(2,1)S(1)}, bf16[2048,6,64]{0,2,1:T(8,128)(2,1)}, u32[]{:S(2)}) copy-start(bf16[2048,6,64]{0,2,1:T(8,128)(2,1)} %get-tuple-element.501) | copy-start | bytes 4718596 | tf_op jit(solution)/shard_map/while
  101.4 12.1 %copy-start.13 = (bf16[4,512,6,64]{1,3,2,0:T(8,128)(2,1)S(1)}, bf16[4,512,6,64]{1,3,2,0:T(8,128)(2,1)}, u32[]{:S(2)}) copy-start(bf16[4,512,6,64]{1,3,2,0:T(8,128)(2,1)} %get-tuple-element.486) | copy-start | bytes 4718596 | tf_op jit(solution)/shard_map/while
  125.2 1.1 copy-start.14
  141.3 12.1 %copy-start.7 = (bf16[2048,6,64]{0,2,1:T(8,128)(2,1)S(1)}, bf16[2048,6,64]{0,2,1:T(8,128)(2,1)}, u32[]{:S(2)}) copy-start(bf16[2048,6,64]{0,2,1:T(8,128)(2,1)} %get-tuple-element.501) | copy-start | bytes 4718596 | tf_op jit(solution)/shard_map/while
  141.3 12.1 %copy-start.13 = (bf16[4,512,6,64]{1,3,2,0:T(8,128)(2,1)S(1)}, bf16[4,512,6,64]{1,3,2,0:T(8,128)(2,1)}, u32[]{:S(2)}) copy-start(bf16[4,512,6,64]{1,3,2,0:T(8,128)(2,1)} %get-tuple-element.486) | copy-start | bytes 4718596 | tf_op jit(solution)/shard_map/while
  165.1 1.1 copy-start.14
  181.2 12.1 %copy-start.7 = (bf16[2048,6,64]{0,2,1:T(8,128)(2,1)S(1)}, bf16[2048,6,64]{0,2,1:T(8,128)(2,1)}, u32[]{:S(2)}) copy-start(bf16[2048,6,64]{0,2,1:T(8,128)(2,1)} %get-tuple-element.501) | copy-start | bytes 4718596 | tf_op jit(solution)/shard_map/while
  181.2 12.1 %copy-start.13 = (bf16[4,512,6,64]{1,3,2,0:T(8,128)(2,1)S(1)}, bf16[4,512,6,64]{1,3,2,0:T(8,128)(2,1)}, u32[]{:S(2)}) copy-start(bf16[4,512,6,64]{1,3,2,0:T(8,128)(2,1)} %get-tuple-element.486) | copy-start | bytes 4718596 | tf_op jit(solution)/shard_map/while
  204.9 1.1 copy-start.14
  206.3 4.3 copy-start.47
  209.4 1.2 copy-start.15
  214.1 12.3 %copy-start.21 = (f32[768]{0:T(1024)S(1)}, f32[768]{0:T(1024)}, u32[]{:S(2)}) copy-start(f32[768]{0:T(1024)} %get-tuple-element.278) | copy-start | bytes 9220
  214.1 67.6 %all-gather.8.cloned.1.call-start = ((), (), s32[]{:S(2)}) async-start(), calls=%async_computation.6 | async-start | bytes 4718592 | tf_op jit(solution)/shard_map/all_gather | solution.py:115
  226.4 2.6 copy-start.4
  226.4 2.8 copy-start.8
  226.4 3.7 copy-start.26
  226.4 3.7 copy-start.36
  230.1 2.8 copy-start.42
  232.1 49.6 %copy-start.48 = (f32[1536]{0:T(1024)S(1)}, f32[1536]{0:T(1024)}, u32[]{:S(2)}) copy-start(f32[1536]{0:T(1024)} %param.26) | copy-start | bytes 18436
  232.2 63.3 %all-gather.10.cloned.1.call-start = ((), (), s32[]{:S(2)}) async-start(), calls=%async_computation.8 | async-start | bytes 4718592 | tf_op jit(solution)/shard_map/all_gather | solution.py:128
  281.6 54.1 %reduce-scatter.9.cloned.1.call-start = ((), (), s32[]{:S(2)}) async-start(), calls=%async_computation.9 | async-start | bytes 4718592 | tf_op jit(solution)/shard_map/reduce_scatter | solution.py:139
  314.9 2.6 copy-start.49
  323.9 1.7 copy-start.46
  323.9 21.7 %reduce-scatter.7.cloned.1.call-start = ((), (), s32[]{:S(2)}) async-start(), calls=%async_computation.7 | async-start | bytes 4718592 | tf_op jit(solution)/shard_map/reduce_scatter | solution.py:120
  335.2 1.4 copy-start.5
  335.2 32.4 %all-gather.12.cloned.1.call-start = ((), (), s32[]{:S(2)}) async-start(), calls=%async_computation.10 | async-start | bytes 4718592 | tf_op jit(solution)/shard_map/all_gather | solution.py:149
  336.6 3.9 copy-start.12
  340.5 5.1 copy-start.33
  351.2 1.7 copy-start.9
  354.2 499.0 %reduce-scatter.11.cloned.1.call-start = ((), (), s32[]{:S(2)}) async-start(), calls=%async_computation.11 | async-start | bytes 4718592 | tf_op jit(solution)/shard_map/reduce_scatter | solution.py:210
  376.6 4.4 copy-start.2
  720.9 5.0 copy-start.10
  741.1 429.4 %all-reduce.5.cloned.1.call-start = ((), (), s32[]{:S(2)}) async-start(), calls=%async_computation.12 | async-start | bytes 28311552 | tf_op jit(solution)/shard_map/psum | solution.py:234
  741.2 9.8 copy-start.44
  750.9 9.1 copy-start.16
  750.9 9.1 copy-start.45
  760.0 2.4 copy-start.17
  760.0 2.4 copy-start.18
  760.0 2.4 copy-start.19
  760.1 3.7 copy-start.43
  769.5 0.7 copy-start.31
  769.6 2.5 copy-start.38
  769.6 83.7 %copy-start.6 = (bf16[1024,768]{1,0:T(8,128)(2,1)S(1)}, bf16[1024,768]{1,0:T(8,128)(2,1)}, u32[]{:S(2)}) copy-start(bf16[1024,768]{1,0:T(8,128)(2,1)} %param.16) | copy-start | bytes 4718596
  769.6 83.7 %copy-start.23 = (f32[1024]{0:T(1024)S(1)}, f32[1024]{0:T(1024)}, u32[]{:S(2)}) copy-start(f32[1024]{0:T(1024)} %copy-done.22) | copy-start | bytes 12292
  769.6 83.6 %copy-start.25 = (f32[768]{0:T(1024)S(1)}, f32[768]{0:T(1024)}, u32[]{:S(2)}) copy-start(f32[768]{0:T(1024)} %copy-done.24) | copy-start | bytes 9220
  769.6 86.3 %copy-start.30 = (f32[1024]{0:T(1024)S(1)}, f32[1024]{0:T(1024)}, u32[]{:S(2)}) copy-start(f32[1024]{0:T(1024)} %copy-done.29) | copy-start | bytes 12292
  769.6 86.3 %copy-start.28 = (f32[1024]{0:T(1024)S(1)}, f32[1024]{0:T(1024)}, u32[]{:S(2)}) copy-start(f32[1024]{0:T(1024)} %copy-done.27) | copy-start | bytes 12292
  853.2 2.7 copy-start.11
  1170.5 5.3 copy-start.20
  1175.8 6.5 slice-start
  1176.8 5.5 slice-start.1
  1176.8 7.7 copy-start.1
  (6 other events, 3.9 us)
Sparse Core Ops, SparseCore 0:
  14.9 14.8 all-gather.5
  214.3 12.0 reduce-scatter.4
  232.3 13.2 all-gather.7
  281.8 7.9 all-gather.9
  324.0 6.7 reduce-scatter.8
  335.4 10.2 reduce-scatter.6
  354.3 13.2 all-gather.11
  741.2 12.0 reduce-scatter.10
  769.7 400.7 all-reduce.4
